TPU v7x, 32 devices: a whole 2x2x4 slice. The times are simulated.
32 devices in a mesh: row: 8 (over z, y), col: 4 (over x, core).
Axes of the slice: x: 2, y: 2, z: 4, core: 2. Of those that a mesh axis runs over, the one named last changes fastest.
Arguments:
- pair_rep: bfloat16 [1024, 1024, 128], P('row', 'col'), may hold values from -8 to 8
- row_ids: int32 [16], P('row'), may hold values from 0 to 1023, as said below
- pad_mask: int32 [1024], P('col'), may hold values from 0 to 1, as said below
- ln_gain: float32 [128], replicated, may hold values from 0.25 to 1.75
- ln_bias: float32 [128], replicated, may hold values from -2 to 2
- w_query: bfloat16 [128, 128], replicated, may hold values from -2 to 2
- w_key: bfloat16 [128, 128], replicated, may hold values from -2 to 2
- w_value: bfloat16 [128, 128], replicated, may hold values from -0.5 to 0.5
- w_gate: bfloat16 [128, 128], replicated, may hold values from -0.5 to 0.5
- gate_bias: float32 [128], replicated, may hold values from -4 to 4
- w_bias: bfloat16 [128, 4], replicated, may hold values from -0.5 to 0.5
- w_out: bfloat16 [128, 128], replicated, may hold values from -0.5 to 0.5
Outputs:
- update: bfloat16 [16, 1024, 128], P('col', 'row')
Inputs may be any that keep to these rules, and one draw needn't show every extreme that they name: `row_ids`: entries t * 2 to t * 2 + 1 are distinct and lie in [t * 128, (t + 1) * 128). `pad_mask`: A prefix of the tokens is real and the rest is padding; the first 257 tokens are real.
All inputs are finite; a program needn't handle non-finite values.
Results may differ from a plain program's by a relative error of at most 0.023.
Values may be sent and summed in bfloat16 or wider, within the bound.
A program may use at most 128 MiB of HBM per device.

v0:
```python
import jax
import jax.numpy as jnp
from jax import lax
from jax.sharding import PartitionSpec as P


def from_root(value, axis, source):
    kept = jnp.where(lax.axis_index(axis) == source, value, 0).astype(value.dtype)
    return lax.psum(kept, axis)


def merged(value, axis, join):
    gathered = jax.tree.map(
        lambda a, kind: lax.all_gather(a.astype(kind), axis),
        value,
        (jnp.bfloat16, jnp.bfloat16, jnp.bfloat16),
    )

    def take(source):
        return jax.tree.map(
            lambda a, own: lax.dynamic_index_in_dim(a, source, 0, False).astype(own.dtype),
            gathered,
            value,
        )

    return lax.fori_loop(
        1, lax.axis_size(axis), lambda source, state: join(state, take(source)), take(0)
    )


def layer_norm(values, ln_gain, ln_bias):
    values = values.astype(jnp.float32)
    centre = jnp.mean(values, axis=-1, keepdims=True)
    spread = jnp.mean((values - centre) ** 2, axis=-1, keepdims=True)
    return ((values - centre) * lax.rsqrt(spread + 1e-05) * ln_gain + ln_bias).astype(jnp.bfloat16)


def project(normed, weight):
    flat = normed.reshape(-1, normed.shape[-1])
    return jnp.dot(flat, weight, preferred_element_type=jnp.float32).reshape(
        normed.shape[:-1] + (weight.shape[1],)
    )


def query_gate(normed, w_query, w_gate, gate_bias, head_dim):
    query = (project(normed, w_query) / jnp.sqrt(jnp.float32(head_dim))).astype(jnp.bfloat16)
    gate = jax.nn.sigmoid(project(normed, w_gate) + gate_bias).astype(jnp.bfloat16)
    return jnp.concatenate([query, gate], axis=-1)


def key_value(normed, w_key, w_value):
    return jnp.concatenate(
        [
            project(normed, w_key).astype(jnp.bfloat16),
            project(normed, w_value).astype(jnp.bfloat16),
        ],
        axis=-1,
    )


def combine_parts(first, second):
    peak_a, total_a, summed_a = first
    peak_b, total_b, summed_b = second
    peak = jnp.maximum(peak_a, peak_b)
    scale_a = jnp.exp(peak_a - peak)
    scale_b = jnp.exp(peak_b - peak)
    return (
        peak,
        total_a * scale_a + total_b * scale_b,
        summed_a * scale_a[..., None] + summed_b * scale_b[..., None],
    )


def body(
    pair_rep,
    row_ids,
    pad_mask,
    ln_gain,
    ln_bias,
    w_query,
    w_key,
    w_value,
    w_gate,
    gate_bias,
    w_bias,
    w_out,
):
    rows_here = pair_rep.shape[0]
    cols_here = pair_rep.shape[1]
    heads = w_bias.shape[1]
    width = w_query.shape[1]
    head_dim = width // heads
    n_col = lax.axis_size("col")
    row_index = lax.axis_index("row")
    col_index = lax.axis_index("col")
    normed = layer_norm(pair_rep, ln_gain, ln_bias)
    offsets = row_ids - row_index * rows_here
    slice_start = row_index * rows_here % cols_here
    root_col = row_index * rows_here // cols_here
    raw_chosen = jnp.take(pair_rep, offsets, axis=0)
    raw_all = lax.all_gather(raw_chosen, "row", axis=0, tiled=True)
    keys_values = key_value(layer_norm(raw_all, ln_gain, ln_bias), w_key, w_value)
    raw_mine = lax.dynamic_slice_in_dim(raw_all, slice_start, rows_here, 1)
    raw_mine = from_root(raw_mine, "col", root_col)
    query_gates = query_gate(
        layer_norm(raw_mine, ln_gain, ln_bias), w_query, w_gate, gate_bias, head_dim
    )
    selected = query_gates.shape[0]
    pair_bias = jnp.einsum("jkc,ch->hjk", normed, w_bias, preferred_element_type=jnp.float32)
    key_live = pad_mask > 0
    query = query_gates[..., :width].reshape(4, selected // 4, rows_here, heads, head_dim)
    gate = query_gates[..., width:]
    key_rows = keys_values[..., :width].reshape(4, selected // 4, cols_here, heads, head_dim)
    value_rows = keys_values[..., width:].reshape(4, selected // 4, cols_here, heads, head_dim)

    def partial_block(items):
        query_block, key_block, value_block = items
        scores = jnp.einsum(
            "tjhd,tkhd->thjk", query_block, key_block, preferred_element_type=jnp.float32
        )
        scores = scores + pair_bias[None]
        scores = jnp.where(key_live[None, None, None, :], scores, jnp.float32(-1000000000.0))
        peak = jnp.max(scores, axis=-1)
        expo = jnp.exp(scores - peak[..., None])
        totals = jnp.sum(expo, axis=-1)
        summed = jnp.einsum(
            "thjk,tkhd->thjd",
            expo.astype(jnp.bfloat16),
            value_block,
            preferred_element_type=jnp.float32,
        )
        return (peak, totals, summed)

    peak, totals, summed = lax.map(partial_block, (query, key_rows, value_rows))
    peak = peak.reshape(selected, heads, rows_here)
    totals = totals.reshape(selected, heads, rows_here)
    summed = summed.reshape(selected, heads, rows_here, head_dim)
    row_count = selected // n_col
    peak, totals, summed = merged((peak, totals, summed), "col", combine_parts)
    totals = lax.dynamic_slice_in_dim(totals, col_index * row_count, row_count, 0)
    summed = lax.dynamic_slice_in_dim(summed, col_index * row_count, row_count, 0)
    attended = summed / totals[..., None]
    attended = jnp.transpose(attended, (0, 2, 1, 3)).reshape(row_count, rows_here, width)
    gate_mine = lax.dynamic_slice_in_dim(gate, col_index * row_count, row_count, 0)
    gated = (gate_mine.astype(jnp.float32) * attended).astype(jnp.bfloat16)
    return project(gated, w_out).astype(jnp.bfloat16)


def solution(mesh):
    return jax.shard_map(
        body,
        mesh=mesh,
        in_specs=(
            P("row", "col", None),
            P("row"),
            P("col"),
            P(),
            P(),
            P(),
            P(),
            P(),
            P(),
            P(),
            P(),
            P(),
        ),
        out_specs=P("col", "row", None),
        check_vma=False,
    )
```

profile of v0, /device:TPU:0, one launch (start us, length us, event | category | flops | bytes accessed | tf_op | source)
XLA Modules:
  0.0 170.1 jit_solution(14934871690667444920)
XLA Ops:
  6.5 0.7 compare_and_fusion
  7.2 4.0 %gather_fusion = bf16[2,256,128]{2,1,0:T(8,128)(2,1)S(1)} fusion(bf16[128,256,128]{2,1,0:T(8,128)(2,1)} %param.16, s32[1024]{0:T(1024)S(1)} %pad_clamp_fusion), kind=kCustom, calls=%fused_computation | custom fusion | bytes 262152 | tf_op jit(solution)/shard_map/jit(_take)/gather | solution.py:100
  11.2 0.7 broadcast_select_fusion
  12.0 5.7 %convert_reduce_fusion = f32[128,256]{1,0:T(8,128)S(1)} fusion(bf16[128,256,128]{2,1,0:T(8,128)(2,1)} %param.16), kind=kLoop, calls=%fused_computation.37 | loop fusion | flops 8355840 | bytes 8519680 | tf_op jit(solution)/shard_map/reduce_sum | solution.py:33
  17.8 10.7 %fusion.23 = f32[128,256]{1,0:T(8,128)S(1)} fusion(bf16[128,256,128]{2,1,0:T(8,128)(2,1)} %param.16, f32[128,256]{1,0:T(8,128)S(1)} %broadcast_multiply_fusion), kind=kLoop, calls=%fused_computation.40 | loop fusion | flops 16744448 | bytes 8650752 | tf_op jit(solution)/shard_map/reduce_sum | solution.py:34
  28.6 11.4 %fusion.38 = f32[4,128,256]{2,0,1:T(4,128)S(1)} fusion(bf16[128,256,128]{2,1,0:T(8,128)(2,1)} %param.16, f32[128]{0:T(128)S(1)} %copy-done.5, f32[128]{0:T(128)S(1)} %copy-done.6, f32[128,256]{1,0:T(8,128)S(1)} %add_rsqrt_fusion, f32[128,256]{1,0:T(8,128)S(1)} %broadcast_multiply_fusion, bf16[128,4]{0,1:T(4,128)(2,1)S(1)} %copy-done.10), kind=kOutput, calls=%fused_computation.61 | convolution fusion | flops 58720256 | bytes 9177088 | tf_op jit(solution)/shard_map/jkc,ch->hjk/dot_general | solution.py:109
  40.1 15.1 %all-gather.3.cloned.1.call-done = bf16[16,256,128]{2,1,0:T(8,128)(2,1)} async-done(((bf16[2,256,128]{2,1,0:T(8,128)(2,1)}), bf16[16,256,128]{2,1,0:T(8,128)(2,1)}) %all-gather.3.cloned.1.call-update) | async-done | bytes 1048592 | tf_op jit(solution)/shard_map/all_gather | solution.py:101
  55.2 2.1 %dynamic-slice_select_fusion = bf16[16,128,128]{2,1,0:T(8,128)(2,1)} fusion(bf16[16,256,128]{2,1,0:T(8,128)(2,1)} %all-gather.3.cloned.1.call-done, s32[]{:T(128)S(6)} %select_n.62, pred[]{:T(512)S(6)} %eq.5), kind=kLoop, calls=%fused_computation.69 | loop fusion | flops 262144 | bytes 1048581 | tf_op jit(solution)/shard_map/jit(_where)/select_n | solution.py:8
  57.3 0.3 convert_reduce_fusion.1
  57.7 1.3 fusion.31
  59.0 1.7 convolution_convert_fusion.1
  60.7 2.5 %convolution_convert_fusion = bf16[16,256,128]{1,2,0:T(8,128)(2,1)} fusion(bf16[16,256,128]{2,1,0:T(8,128)(2,1)S(1)} %copy-done.1, f32[128]{0:T(128)S(1)} %copy-done.5, f32[128]{0:T(128)S(1)} %copy-done.6, f32[16,256]{1,0:T(8,128)S(1)} %add_rsqrt_fusion.1, f32[16,256]{1,0:T(8,128)S(1)} %broadcast_multiply_fusion.1, bf16[128,128]{1,0:T(8,128)(2,1)S(1)} %copy-done.7), kind=kOutput, calls=%fused_computation.53 | convolution fusion | flops 137887744 | bytes 2163712 | tf_op jit(solution)/shard_map/dot_general | solution.py:40
  63.2 26.5 %all-reduce.2.cloned.1.call-done = bf16[16,128,128]{2,1,0:T(8,128)(2,1)} async-done(((bf16[16,128,128]{2,1,0:T(8,128)(2,1)}), bf16[16,128,128]{2,1,0:T(8,128)(2,1)}) %all-reduce.2.cloned.1.call-update) | async-done | bytes 524304 | tf_op jit(solution)/shard_map/psum | solution.py:9
  89.7 1.2 convert_reduce_fusion.2
  91.0 1.7 fusion.41
  92.7 1.9 %fusion.35 = bf16[16,128,128]{1,2,0:T(8,128)(2,1)S(1)} fusion(bf16[16,128,128]{2,1,0:T(8,128)(2,1)} %all-reduce.2.cloned.1.call-done, f32[128]{0:T(128)S(1)} %copy-done.5, f32[128]{0:T(128)S(1)} %copy-done.6, f32[16,128]{1,0:T(8,128)S(1)} %add_rsqrt_fusion.2, f32[16,128]{1,0:T(8,128)S(1)} %broadcast_multiply_fusion.2, bf16[128,128]{1,0:T(8,128)(2,1)S(1)} %copy-done.8), kind=kOutput, calls=%fused_computation.58 | convolution fusion | flops 69206016 | bytes 1098752 | tf_op jit(solution)/shard_map/dot_general | solution.py:40
  94.6 12.7 %while.33 = (s32[]{:T(128)}, bf16[4,4,4,128]{3,2,1,0:T(4,128)(2,1)S(1)}, bf16[4,4,4,128]{3,2,1,0:T(4,128)(2,1)S(1)}, bf16[4,4,4,128,32]{3,4,2,1,0:T(8,128)(2,1)S...) while((s32[]{:T(128)}, ...), condition=%wide.region_10.11_spmd, body=%wide.region_7.10_spmd.sunk | while | flops 72871936 | bytes 8838517 | solution.py:134
  94.6 0.6 fusion.76
  95.2 0.9 fusion.77
  96.1 1.6 fusion.78
  97.8 0.6 fusion.76
  98.4 0.9 fusion.77
  99.3 1.6 fusion.78
  100.9 0.6 fusion.76
  101.5 0.9 fusion.77
  102.5 1.6 fusion.78
  104.1 0.6 fusion.76
  104.7 0.9 fusion.77
  105.6 1.6 fusion.78
  107.3 0.8 copy-done.3
  108.1 5.2 %all_gather.16 = bf16[4,16,4,128]{3,1,2,0:T(8,128)(2,1)S(1)} all-gather(bf16[1,16,4,128]{3,1,2,0:T(8,128)(2,1)S(1)} %bitcast.102), channel_id=1, replica_groups=mesh['row'=8,'col'=4] {'col'}, dimensions={0}, use_global_device_ids=true | all-gather | bytes 81920 | tf_op jit(solution)/shard_map/all_gather | solution.py:14
  113.4 5.4 %all_gather.17 = bf16[4,16,4,128]{3,1,2,0:T(8,128)(2,1)S(1)} all-gather(bf16[1,16,4,128]{3,1,2,0:T(8,128)(2,1)S(1)} %bitcast.103), channel_id=1, replica_groups=mesh['row'=8,'col'=4] {'col'}, dimensions={0}, use_global_device_ids=true | all-gather | bytes 81920 | tf_op jit(solution)/shard_map/all_gather | solution.py:14
  118.9 1.7 %fusion.49 = f32[16,128,128]{2,1,0:T(8,128)} fusion(bf16[16,128,128]{2,1,0:T(8,128)(2,1)S(1)} %copy-done.2, f32[128]{0:T(128)S(1)} %copy-done.5, f32[128]{0:T(128)S(1)} %copy-done.6, f32[16,128]{1,0:T(8,128)S(1)} %add_rsqrt_fusion.2, f32[16,128]{1,0:T(8,128)S(1)} %broadcast_multiply_fusion.2, bf16[128,128]{1,0:T(8,128)(2,1)S(1)} %copy-done.4), kind=kOutput, calls=%fused_computation.70 | convolution fusion | flops 68681728 | bytes 1623040 | tf_op jit(solution)/shard_map/dot_general | solution.py:40
  120.6 10.3 %all-gather.5.cloned.1.call-done = bf16[4,16,4,128,32]{3,4,2,1,0:T(8,128)(2,1)} async-done(((bf16[1,16,4,128,32]{3,4,2,1,0:T(8,128)(2,1)}), bf16[4,16,4,128,32]{3,4,2,1,0:T(8,128)(2,1)}) %all-gather.5.cloned.1.call-update) | async-done | bytes 2097168 | tf_op jit(solution)/shard_map/all_gather | solution.py:14
  130.9 1.2 fusion.47
  132.1 2.6 %copy.33 = f32[16,4,128,32]{3,2,1,0:T(8,128)} copy(f32[16,4,128,32]{2,3,1,0:T(8,128)S(1)} %fusion.47) | data formatting | bytes 2097152 | tf_op jit(solution)/shard_map/while | solution.py:26
  134.7 24.0 %while.34 = (s32[]{:T(128)}, f32[16,4,128]{2,1,0:T(4,128)S(1)}, f32[16,4,128]{2,1,0:T(4,128)S(1)}, f32[16,4,128,32]{3,2,1,0:T(8,128)}, bf16[4,16,4,128]{3,1,2,0:...) while((s32[]{:T(128)}, f32[16,4,128]{2,1,0:T(4,128)S(1)}, ...), condition=%wide.region_12.13_spmd, body=%wide.region_11.12_spmd.sunk | while | flops 1114117 | bytes 5079191 | solution.py:26
  134.8 1.1 constant_dynamic-slice_fusion.7
  135.9 1.0 copy.61
  136.9 5.8 %fusion.80 = f32[16,4,128,32]{3,2,1,0:T(8,128)} fusion(f32[16,4,128,32]{3,2,1,0:T(8,128)} %get-tuple-element.469, bf16[1,16,4,128,32]{4,3,2,1,0:T(8,128)(2,1)S(1)} %copy.61, f32[16,4,128]{2,1,0:T(4,128)S(1)} %get-tuple-element.424, f32[16,4,128]{2,1,0:T(4,128)S(1)} %get-tuple-element.425), kind=kLoop, calls=%fused_computation.24.clone.1 | loop fusion | flops 1048576 | bytes 2686976 | tf_op jit(solution)/shard_map/while/body/eval_jaxpr/add | solution.py:70
  142.8 1.1 constant_dynamic-slice_fusion.7
  143.9 1.0 copy.61
  145.0 5.8 %fusion.80 = f32[16,4,128,32]{3,2,1,0:T(8,128)} fusion(f32[16,4,128,32]{3,2,1,0:T(8,128)} %get-tuple-element.469, bf16[1,16,4,128,32]{4,3,2,1,0:T(8,128)(2,1)S(1)} %copy.61, f32[16,4,128]{2,1,0:T(4,128)S(1)} %get-tuple-element.424, f32[16,4,128]{2,1,0:T(4,128)S(1)} %get-tuple-element.425), kind=kLoop, calls=%fused_computation.24.clone.1 | loop fusion | flops 1048576 | bytes 2686976 | tf_op jit(solution)/shard_map/while/body/eval_jaxpr/add | solution.py:70
  150.8 1.1 constant_dynamic-slice_fusion.7
  151.9 1.0 copy.61
  153.0 5.8 %fusion.80 = f32[16,4,128,32]{3,2,1,0:T(8,128)} fusion(f32[16,4,128,32]{3,2,1,0:T(8,128)} %get-tuple-element.469, bf16[1,16,4,128,32]{4,3,2,1,0:T(8,128)(2,1)S(1)} %copy.61, f32[16,4,128]{2,1,0:T(4,128)S(1)} %get-tuple-element.424, f32[16,4,128]{2,1,0:T(4,128)S(1)} %get-tuple-element.425), kind=kLoop, calls=%fused_computation.24.clone.1 | loop fusion | flops 1048576 | bytes 2686976 | tf_op jit(solution)/shard_map/while/body/eval_jaxpr/add | solution.py:70
  158.8 2.8 %copy.37 = f32[16,4,128,32]{2,3,1,0:T(8,128)S(1)} copy(f32[16,4,128,32]{3,2,1,0:T(8,128)} %get-tuple-element.234) | data formatting | bytes 2097152 | tf_op jit(solution)/shard_map/while | solution.py:26
  161.8 1.8 %convolution_convert_fusion.2 = bf16[4,128,128]{2,1,0:T(8,128)(2,1)} fusion(f32[4,128,128]{2,1,0:T(8,128)S(1)} %copy.38, f32[16,128,128]{2,1,0:T(8,128)} %fusion.49, s32[]{:T(128)S(6)} %select_n.64, f32[128]{0:T(128)S(1)} %copy-done.12, bf16[128,128]{1,0:T(8,128)(2,1)S(1)} %copy-done.9), kind=kOutput, calls=%fused_computation.62 | convolution fusion | flops 17367040 | bytes 688644 | tf_op jit(solution)/shard_map/dot_general | solution.py:40
  (66 shorter events, 0.9 us)
Async XLA Ops:
  6.5 52.5 %copy-start = (bf16[128,128]{1,0:T(8,128)(2,1)S(1)}, bf16[128,128]{1,0:T(8,128)(2,1)}, u32[]{:S(2)}) copy-start(bf16[128,128]{1,0:T(8,128)(2,1)} %param.22) | copy-start | bytes 98308
  6.5 48.6 %all-gather.3.cloned.1.call-start = ((), (), s32[]{:S(2)}) async-start(), calls=%async_computation | async-start | bytes 1179648 | tf_op jit(solution)/shard_map/all_gather | solution.py:101
  11.9 77.8 %all-reduce.2.cloned.1.call-start = ((), (), s32[]{:S(2)}) async-start(), calls=%async_computation.1 | async-start | bytes 1048576 | tf_op jit(solution)/shard_map/psum | solution.py:9
  17.7 10.8 %copy-start.5 = (f32[128]{0:T(128)S(1)}, f32[128]{0:T(128)}, u32[]{:S(2)}) copy-start(f32[128]{0:T(128)} %param.20) | copy-start | bytes 1540
  17.7 10.8 %copy-start.6 = (f32[128]{0:T(128)S(1)}, f32[128]{0:T(128)}, u32[]{:S(2)}) copy-start(f32[128]{0:T(128)} %param.19) | copy-start | bytes 1540
  17.8 10.8 %copy-start.10 = (bf16[128,4]{0,1:T(4,128)(2,1)S(1)}, bf16[128,4]{0,1:T(4,128)(2,1)}, u32[]{:S(2)}) copy-start(bf16[128,4]{0,1:T(4,128)(2,1)} %param.26) | copy-start | bytes 3076
  28.6 11.5 %copy-start.11 = (s32[256]{0:T(256)S(1)}, s32[256]{0:T(256)}, u32[]{:S(2)}) copy-start(s32[256]{0:T(256)} %param.18) | copy-start | bytes 3076
  55.2 2.1 %copy-start.1 = (bf16[16,256,128]{2,1,0:T(8,128)(2,1)S(1)}, bf16[16,256,128]{2,1,0:T(8,128)(2,1)}, u32[]{:S(2)}) copy-start(bf16[16,256,128]{2,1,0:T(8,128)(2,1)} %all-gather.3.cloned.1.call-done) | copy-start | bytes 3145732
  57.3 73.7 %all-gather.5.cloned.1.call-start = ((), (), s32[]{:S(2)}) async-start(), calls=%async_computation.2 | async-start | bytes 2621440 | tf_op jit(solution)/shard_map/all_gather | solution.py:14
  57.7 3.0 %copy-start.7 = (bf16[128,128]{1,0:T(8,128)(2,1)S(1)}, bf16[128,128]{1,0:T(8,128)(2,1)}, u32[]{:S(2)}) copy-start(bf16[128,128]{1,0:T(8,128)(2,1)} %param.23) | copy-start | bytes 98308
  60.7 31.9 %copy-start.8 = (bf16[128,128]{1,0:T(8,128)(2,1)S(1)}, bf16[128,128]{1,0:T(8,128)(2,1)}, u32[]{:S(2)}) copy-start(bf16[128,128]{1,0:T(8,128)(2,1)} %param.21) | copy-start | bytes 98308
  94.5 24.3 %copy-start.2 = (bf16[16,128,128]{2,1,0:T(8,128)(2,1)S(1)}, bf16[16,128,128]{2,1,0:T(8,128)(2,1)}, u32[]{:S(2)}) copy-start(bf16[16,128,128]{2,1,0:T(8,128)(2,1)} %all-reduce.2.cloned.1.call-done) | copy-start | bytes 1572868
  94.6 24.3 %copy-start.4 = (bf16[128,128]{1,0:T(8,128)(2,1)S(1)}, bf16[128,128]{1,0:T(8,128)(2,1)}, u32[]{:S(2)}) copy-start(bf16[128,128]{1,0:T(8,128)(2,1)} %param.24) | copy-start | bytes 98308
  107.3 0.8 copy-start.3
  158.8 3.0 %copy-start.9 = (bf16[128,128]{1,0:T(8,128)(2,1)S(1)}, bf16[128,128]{1,0:T(8,128)(2,1)}, u32[]{:S(2)}) copy-start(bf16[128,128]{1,0:T(8,128)(2,1)} %param.27) | copy-start | bytes 98308
  158.8 3.0 %copy-start.12 = (f32[128]{0:T(128)S(1)}, f32[128]{0:T(128)}, u32[]{:S(2)}) copy-start(f32[128]{0:T(128)} %param.25) | copy-start | bytes 1540
Sparse Core Ops, SparseCore 0:
  12.1 43.0 all-gather.2
  57.5 32.1 all-reduce.1
  108.2 22.6 all-gather.4
where the time goes:
time: 171 us; the launch traced here: 170 us
  waiting for transfers between devices  52 us (30%)
  other arithmetic  46.9 us (27%)
  matrix products  29.8 us (17%)
  local copies, waits for them, and re-layouts  17 us (10%)
  between operations  13.5 us (8%)
  blocking collectives  10.7 us (6%)
    psum x1, waiting for transfers between devices, from_root(): return lax.psum(kept, axis)  26.5 us
    add x3, other arithmetic, combine_parts(): summed_a * scale_a[..., None] + summed_b * scale_b[..., None]  17.4 us
    all_gather x1, waiting for transfers between devices, body(): raw_all = lax.all_gather(raw_chosen, 'row', axis=0, tiled=True)  15.1 us
    reduce_sum x3, other arithmetic, layer_norm(): spread = jnp.mean((values - centre) ** 2, axis=-1, keepdims=True)  13.7 us
    dot_general x1, matrix products, body(): jnp.einsum('jkc,ch->hjk', normed, w_bias, preferred_element_type=jnp.floa...  11.4 us
    all_gather x2, blocking collectives, merged(): lax.all_gather(a.astype(kind), axis)  10.7 us
    all_gather x1, waiting for transfers between devices, merged(): lax.all_gather(a.astype(kind), axis)  10.3 us
    dot_general x5, matrix products, project(): jnp.dot(flat, weight, preferred_element_type=jnp.float32)  9.55 us
  transfers between devices with their start and end apart: 3, of which 3 were waited for; matrix products, arithmetic and copies ran while one was open for 21% of the time, Pallas kernels for 0%

commit v1 on v0

--- a/solution.py
+++ b/solution.py
@@ -6,7 +6,7 @@
 
 def from_root(value, axis, source):
     kept = jnp.where(lax.axis_index(axis) == source, value, 0).astype(value.dtype)
-    return lax.psum(kept, axis)
+    return jnp.sum(lax.all_gather(kept, axis), axis=0)
 
 
 def merged(value, axis, join):

time: 171 us -> 165 us (0.965)
  waiting for transfers between devices: 52 us -> 46.5 us
    psum x1 -> x0, waiting for transfers between devices: 26.5 us -> none  [from_root(): return lax.psum(kept, axis)]
    all_gather x1, waiting for transfers between devices: 15.1 us -> 37.4 us  [body(): raw_all = lax.all_gather(raw_chosen, 'row', axis=0, tiled=True)]
    reduce_sum x0 -> x1, other arithmetic: none -> 2.03 us  [from_root(): return jnp.sum(lax.all_gather(kept, axis), axis=0)]
  transfers between devices with their start and end apart: 3 -> 3, of which waited for: 3 -> 2; matrix products, arithmetic and copies ran while one was open for 21% -> 22% of each run, Pallas kernels for 0% -> 0%
where the time goes in v1:
time: 165 us; the launch traced here: 164 us
  other arithmetic  46.8 us (28%)
  waiting for transfers between devices  46.5 us (28%)
  matrix products  29.1 us (18%)
  local copies, waits for them, and re-layouts  17 us (10%)
  between operations  13.5 us (8%)
  blocking collectives  10.9 us (7%)
    all_gather x1, waiting for transfers between devices, body(): raw_all = lax.all_gather(raw_chosen, 'row', axis=0, tiled=True)  37.4 us
    add x3, other arithmetic, combine_parts(): summed_a * scale_a[..., None] + summed_b * scale_b[..., None]  17.4 us
    reduce_sum x3, other arithmetic, layer_norm(): spread = jnp.mean((values - centre) ** 2, axis=-1, keepdims=True)  12.6 us
    dot_general x1, matrix products, body(): jnp.einsum('jkc,ch->hjk', normed, w_bias, preferred_element_type=jnp.floa...  11.5 us
    all_gather x2, blocking collectives, merged(): lax.all_gather(a.astype(kind), axis)  10.9 us
    all_gather x1, waiting for transfers between devices, merged(): lax.all_gather(a.astype(kind), axis)  9.09 us
    dot_general x5, matrix products, project(): jnp.dot(flat, weight, preferred_element_type=jnp.float32)  8.85 us
    dot_general x4, matrix products, partial_block(): jnp.einsum('thjk,tkhd->thjd', expo.astype(jnp.bfloat16), value_block, pre...  6.4 us
  transfers between devices with their start and end apart: 3, of which 2 were waited for; matrix products, arithmetic and copies ran while one was open for 22% of the time, Pallas kernels for 0%

profile of v1, /device:TPU:0, one launch (start us, length us, event | category | flops | bytes accessed | tf_op | source)
XLA Modules:
  0.0 164.0 jit_solution(17292548208128399043)
XLA Ops:
  6.5 0.7 compare_and_fusion
  7.2 4.0 %gather_fusion = bf16[2,256,128]{2,1,0:T(8,128)(2,1)S(1)} fusion(bf16[128,256,128]{2,1,0:T(8,128)(2,1)} %param.16, s32[1024]{0:T(1024)S(1)} %pad_clamp_fusion), kind=kCustom, calls=%fused_computation | custom fusion | bytes 262152 | tf_op jit(solution)/shard_map/jit(_take)/gather | solution.py:100
  11.2 0.7 broadcast_select_fusion
  12.1 5.7 %convert_reduce_fusion = f32[128,256]{1,0:T(8,128)S(1)} fusion(bf16[128,256,128]{2,1,0:T(8,128)(2,1)} %param.16), kind=kLoop, calls=%fused_computation.37 | loop fusion | flops 8355840 | bytes 8519680 | tf_op jit(solution)/shard_map/reduce_sum | solution.py:33
  17.7 37.4 %all-gather.5.cloned.1.call-done = bf16[16,256,128]{2,1,0:T(8,128)(2,1)} async-done(((bf16[2,256,128]{2,1,0:T(8,128)(2,1)}), bf16[16,256,128]{2,1,0:T(8,128)(2,1)}) %all-gather.5.cloned.1.call-update) | async-done | bytes 1048592 | tf_op jit(solution)/shard_map/all_gather | solution.py:101
  55.1 2.0 %dynamic-slice_select_fusion = bf16[16,128,128]{2,1,0:T(8,128)(2,1)} fusion(bf16[16,256,128]{2,1,0:T(8,128)(2,1)} %all-gather.5.cloned.1.call-done, s32[]{:T(128)S(6)} %select_n.62, pred[]{:T(512)S(6)} %eq.5), kind=kLoop, calls=%fused_computation.69 | loop fusion | flops 262144 | bytes 1048581 | tf_op jit(solution)/shard_map/jit(_where)/select_n | solution.py:8
  57.2 10.7 %fusion.23 = f32[128,256]{1,0:T(8,128)S(1)} fusion(bf16[128,256,128]{2,1,0:T(8,128)(2,1)} %param.16, f32[128,256]{1,0:T(8,128)S(1)} %broadcast_multiply_fusion), kind=kLoop, calls=%fused_computation.40 | loop fusion | flops 16744448 | bytes 8650752 | tf_op jit(solution)/shard_map/reduce_sum | solution.py:34
  68.0 11.5 %fusion.38 = f32[4,128,256]{2,0,1:T(4,128)S(1)} fusion(bf16[128,256,128]{2,1,0:T(8,128)(2,1)} %param.16, f32[128]{0:T(128)S(1)} %copy-done.4, f32[128]{0:T(128)S(1)} %copy-done.5, f32[128,256]{1,0:T(8,128)S(1)} %add_rsqrt_fusion, f32[128,256]{1,0:T(8,128)S(1)} %broadcast_multiply_fusion, bf16[128,4]{0,1:T(4,128)(2,1)S(1)} %copy-done.9), kind=kOutput, calls=%fused_computation.61 | convolution fusion | flops 58720256 | bytes 9177088 | tf_op jit(solution)/shard_map/jkc,ch->hjk/dot_general | solution.py:109
  79.6 0.3 convert_reduce_fusion.1
  80.0 1.3 fusion.31
  81.3 1.7 %convolution_convert_fusion.1 = bf16[16,256,128]{1,2,0:T(8,128)(2,1)S(1)} fusion(bf16[16,256,128]{2,1,0:T(8,128)(2,1)S(1)} %copy-done.1, f32[128]{0:T(128)S(1)} %copy-done.4, f32[128]{0:T(128)S(1)} %copy-done.5, f32[16,256]{1,0:T(8,128)S(1)} %add_rsqrt_fusion.1, f32[16,256]{1,0:T(8,128)S(1)} %broadcast_multiply_fusion.1, bf16[128,128]{1,0:T(8,128)(2,1)S(1)} %copy-done), kind=kOutput, calls=%fused_computation.54 | convolution fusion | flops 137887744 | bytes 2163712 | tf_op jit(solution)/shard_map/dot_general | solution.py:40
  83.0 2.5 %convolution_convert_fusion = bf16[16,256,128]{1,2,0:T(8,128)(2,1)} fusion(bf16[16,256,128]{2,1,0:T(8,128)(2,1)S(1)} %copy-done.1, f32[128]{0:T(128)S(1)} %copy-done.4, f32[128]{0:T(128)S(1)} %copy-done.5, f32[16,256]{1,0:T(8,128)S(1)} %add_rsqrt_fusion.1, f32[16,256]{1,0:T(8,128)S(1)} %broadcast_multiply_fusion.1, bf16[128,128]{1,0:T(8,128)(2,1)S(1)} %copy-done.6), kind=kOutput, calls=%fused_computation.53 | convolution fusion | flops 137887744 | bytes 2163712 | tf_op jit(solution)/shard_map/dot_general | solution.py:40
  85.5 2.0 %reduce_sum.75 = bf16[16,128,128]{2,1,0:T(8,128)(2,1)S(1)} reduce(bf16[4,16,128,128]{3,2,1,0:T(8,128)(2,1)} %bitcast.99, bf16[]{:T(256)} %constant.148.clone.1), dimensions={0}, to_apply=%region_0.0 | reduce | flops 786432 | bytes 2621442 | tf_op jit(solution)/shard_map/reduce_sum | solution.py:9
  87.5 0.2 convert_reduce_fusion.2
  87.8 0.6 fusion.41
  88.4 1.1 fusion.35
  89.6 12.6 %while.33 = (s32[]{:T(128)}, bf16[4,4,4,128]{3,2,1,0:T(4,128)(2,1)S(1)}, bf16[4,4,4,128]{3,2,1,0:T(4,128)(2,1)S(1)}, bf16[4,4,4,128,32]{3,4,2,1,0:T(8,128)(2,1)S...) while((s32[]{:T(128)}, ...), condition=%wide.region_10.11_spmd, body=%wide.region_7.10_spmd.sunk | while | flops 72871936 | bytes 8838517 | solution.py:134
  89.6 0.6 fusion.76
  90.2 0.9 fusion.77
  91.1 1.6 fusion.78
  92.7 0.6 fusion.76
  93.3 0.9 fusion.77
  94.3 1.6 fusion.78
  95.9 0.6 fusion.76
  96.5 0.9 fusion.77
  97.4 1.6 fusion.78
  99.0 0.6 fusion.76
  99.6 0.9 fusion.77
  100.5 1.6 fusion.78
  102.2 0.8 copy-done.2
  103.0 5.2 %all_gather.24 = bf16[4,16,4,128]{3,1,2,0:T(8,128)(2,1)S(1)} all-gather(bf16[1,16,4,128]{3,1,2,0:T(8,128)(2,1)S(1)} %bitcast.104), channel_id=1, replica_groups=mesh['row'=8,'col'=4] {'col'}, dimensions={0}, use_global_device_ids=true | all-gather | bytes 81920 | tf_op jit(solution)/shard_map/all_gather | solution.py:14
  108.3 5.6 %all_gather.25 = bf16[4,16,4,128]{3,1,2,0:T(8,128)(2,1)S(1)} all-gather(bf16[1,16,4,128]{3,1,2,0:T(8,128)(2,1)S(1)} %bitcast.105), channel_id=1, replica_groups=mesh['row'=8,'col'=4] {'col'}, dimensions={0}, use_global_device_ids=true | all-gather | bytes 81920 | tf_op jit(solution)/shard_map/all_gather | solution.py:14
  113.9 1.7 %fusion.49 = f32[16,128,128]{2,1,0:T(8,128)} fusion(bf16[16,128,128]{2,1,0:T(8,128)(2,1)S(1)} %reduce_sum.75, f32[128]{0:T(128)S(1)} %copy-done.4, f32[128]{0:T(128)S(1)} %copy-done.5, f32[16,128]{1,0:T(8,128)S(1)} %add_rsqrt_fusion.2, f32[16,128]{1,0:T(8,128)S(1)} %broadcast_multiply_fusion.2, bf16[128,128]{1,0:T(8,128)(2,1)S(1)} %copy-done.3), kind=kOutput, calls=%fused_computation.70 | convolution fusion | flops 68681728 | bytes 1623040 | tf_op jit(solution)/shard_map/dot_general | solution.py:40
  115.7 9.1 %all-gather.7.cloned.1.call-done = bf16[4,16,4,128,32]{3,4,2,1,0:T(8,128)(2,1)} async-done(((bf16[1,16,4,128,32]{3,4,2,1,0:T(8,128)(2,1)}), bf16[4,16,4,128,32]{3,4,2,1,0:T(8,128)(2,1)}) %all-gather.7.cloned.1.call-update) | async-done | bytes 2097168 | tf_op jit(solution)/shard_map/all_gather | solution.py:14
  124.8 1.2 fusion.47
  125.9 2.6 %copy.33 = f32[16,4,128,32]{3,2,1,0:T(8,128)} copy(f32[16,4,128,32]{2,3,1,0:T(8,128)S(1)} %fusion.47) | data formatting | bytes 2097152 | tf_op jit(solution)/shard_map/while | solution.py:26
  128.6 24.0 %while.34 = (s32[]{:T(128)}, f32[16,4,128]{2,1,0:T(4,128)S(1)}, f32[16,4,128]{2,1,0:T(4,128)S(1)}, f32[16,4,128,32]{3,2,1,0:T(8,128)}, bf16[4,16,4,128]{3,1,2,0:...) while((s32[]{:T(128)}, f32[16,4,128]{2,1,0:T(4,128)S(1)}, ...), condition=%wide.region_12.13_spmd, body=%wide.region_11.12_spmd.sunk | while | flops 1114117 | bytes 5079191 | solution.py:26
  128.6 1.1 constant_dynamic-slice_fusion.7
  129.7 1.0 copy.61
  130.8 5.8 %fusion.80 = f32[16,4,128,32]{3,2,1,0:T(8,128)} fusion(f32[16,4,128,32]{3,2,1,0:T(8,128)} %get-tuple-element.469, bf16[1,16,4,128,32]{4,3,2,1,0:T(8,128)(2,1)S(1)} %copy.61, f32[16,4,128]{2,1,0:T(4,128)S(1)} %get-tuple-element.424, f32[16,4,128]{2,1,0:T(4,128)S(1)} %get-tuple-element.425), kind=kLoop, calls=%fused_computation.24.clone.1 | loop fusion | flops 1048576 | bytes 2686976 | tf_op jit(solution)/shard_map/while/body/eval_jaxpr/add | solution.py:70
  136.6 1.1 constant_dynamic-slice_fusion.7
  137.7 1.0 copy.61
  138.8 5.8 %fusion.80 = f32[16,4,128,32]{3,2,1,0:T(8,128)} fusion(f32[16,4,128,32]{3,2,1,0:T(8,128)} %get-tuple-element.469, bf16[1,16,4,128,32]{4,3,2,1,0:T(8,128)(2,1)S(1)} %copy.61, f32[16,4,128]{2,1,0:T(4,128)S(1)} %get-tuple-element.424, f32[16,4,128]{2,1,0:T(4,128)S(1)} %get-tuple-element.425), kind=kLoop, calls=%fused_computation.24.clone.1 | loop fusion | flops 1048576 | bytes 2686976 | tf_op jit(solution)/shard_map/while/body/eval_jaxpr/add | solution.py:70
  144.7 1.1 constant_dynamic-slice_fusion.7
  145.7 1.0 copy.61
  146.8 5.8 %fusion.80 = f32[16,4,128,32]{3,2,1,0:T(8,128)} fusion(f32[16,4,128,32]{3,2,1,0:T(8,128)} %get-tuple-element.469, bf16[1,16,4,128,32]{4,3,2,1,0:T(8,128)(2,1)S(1)} %copy.61, f32[16,4,128]{2,1,0:T(4,128)S(1)} %get-tuple-element.424, f32[16,4,128]{2,1,0:T(4,128)S(1)} %get-tuple-element.425), kind=kLoop, calls=%fused_computation.24.clone.1 | loop fusion | flops 1048576 | bytes 2686976 | tf_op jit(solution)/shard_map/while/body/eval_jaxpr/add | solution.py:70
  152.6 2.8 %copy.37 = f32[16,4,128,32]{2,3,1,0:T(8,128)S(1)} copy(f32[16,4,128,32]{3,2,1,0:T(8,128)} %get-tuple-element.234) | data formatting | bytes 2097152 | tf_op jit(solution)/shard_map/while | solution.py:26
  155.6 1.8 %convolution_convert_fusion.2 = bf16[4,128,128]{2,1,0:T(8,128)(2,1)} fusion(f32[4,128,128]{2,1,0:T(8,128)S(1)} %copy.38, f32[16,128,128]{2,1,0:T(8,128)} %fusion.49, s32[]{:T(128)S(6)} %select_n.64, f32[128]{0:T(128)S(1)} %copy-done.11, bf16[128,128]{1,0:T(8,128)(2,1)S(1)} %copy-done.8), kind=kOutput, calls=%fused_computation.62 | convolution fusion | flops 17367040 | bytes 688644 | tf_op jit(solution)/shard_map/dot_general | solution.py:40
  (65 shorter events, 0.9 us)
Async XLA Ops:
  6.5 74.8 %copy-start = (bf16[128,128]{1,0:T(8,128)(2,1)S(1)}, bf16[128,128]{1,0:T(8,128)(2,1)}, u32[]{:S(2)}) copy-start(bf16[128,128]{1,0:T(8,128)(2,1)} %param.22) | copy-start | bytes 98308
  6.5 48.6 %all-gather.5.cloned.1.call-start = ((), (), s32[]{:S(2)}) async-start(), calls=%async_computation | async-start | bytes 1179648 | tf_op jit(solution)/shard_map/all_gather | solution.py:101
  11.9 73.6 %all-gather.9.cloned.1.call-start = ((), (), s32[]{:S(2)}) async-start(), calls=%async_computation.2 | async-start | bytes 2621440 | tf_op jit(solution)/shard_map/all_gather | solution.py:9
  57.1 10.8 %copy-start.4 = (f32[128]{0:T(128)S(1)}, f32[128]{0:T(128)}, u32[]{:S(2)}) copy-start(f32[128]{0:T(128)} %param.20) | copy-start | bytes 1540
  57.1 10.8 %copy-start.5 = (f32[128]{0:T(128)S(1)}, f32[128]{0:T(128)}, u32[]{:S(2)}) copy-start(f32[128]{0:T(128)} %param.19) | copy-start | bytes 1540
  57.1 10.8 %copy-start.9 = (bf16[128,4]{0,1:T(4,128)(2,1)S(1)}, bf16[128,4]{0,1:T(4,128)(2,1)}, u32[]{:S(2)}) copy-start(bf16[128,4]{0,1:T(4,128)(2,1)} %param.26) | copy-start | bytes 3076
  57.1 67.6 %all-gather.7.cloned.1.call-start = ((), (), s32[]{:S(2)}) async-start(), calls=%async_computation.1 | async-start | bytes 2621440 | tf_op jit(solution)/shard_map/all_gather | solution.py:14
  68.0 11.6 %copy-start.10 = (s32[256]{0:T(256)S(1)}, s32[256]{0:T(256)}, u32[]{:S(2)}) copy-start(s32[256]{0:T(256)} %param.18) | copy-start | bytes 3076
  68.0 11.6 %copy-start.1 = (bf16[16,256,128]{2,1,0:T(8,128)(2,1)S(1)}, bf16[16,256,128]{2,1,0:T(8,128)(2,1)}, u32[]{:S(2)}) copy-start(bf16[16,256,128]{2,1,0:T(8,128)(2,1)} %all-gather.5.cloned.1.call-done) | copy-start | bytes 3145732
  79.9 3.1 %copy-start.6 = (bf16[128,128]{1,0:T(8,128)(2,1)S(1)}, bf16[128,128]{1,0:T(8,128)(2,1)}, u32[]{:S(2)}) copy-start(bf16[128,128]{1,0:T(8,128)(2,1)} %param.23) | copy-start | bytes 98308
  85.5 2.9 %copy-start.7 = (bf16[128,128]{1,0:T(8,128)(2,1)S(1)}, bf16[128,128]{1,0:T(8,128)(2,1)}, u32[]{:S(2)}) copy-start(bf16[128,128]{1,0:T(8,128)(2,1)} %param.21) | copy-start | bytes 98308
  89.6 24.4 %copy-start.3 = (bf16[128,128]{1,0:T(8,128)(2,1)S(1)}, bf16[128,128]{1,0:T(8,128)(2,1)}, u32[]{:S(2)}) copy-start(bf16[128,128]{1,0:T(8,128)(2,1)} %param.24) | copy-start | bytes 98308
  102.2 0.8 copy-start.2
  152.6 3.0 %copy-start.8 = (bf16[128,128]{1,0:T(8,128)(2,1)S(1)}, bf16[128,128]{1,0:T(8,128)(2,1)}, u32[]{:S(2)}) copy-start(bf16[128,128]{1,0:T(8,128)(2,1)} %param.27) | copy-start | bytes 98308
  152.6 3.0 %copy-start.11 = (f32[128]{0:T(128)S(1)}, f32[128]{0:T(128)}, u32[]{:S(2)}) copy-start(f32[128]{0:T(128)} %param.25) | copy-start | bytes 1540
Sparse Core Ops, SparseCore 0:
  12.1 42.9 all-gather.4
  57.2 21.2 all-gather.8
  103.1 21.6 all-gather.6
